TPU v7x, 32 devices: a whole 2x2x4 slice. The times are simulated.
32 devices in a mesh: dp: 8 (over z, x), narrow: 4 (over y, core).
Axes of the slice: x: 2, y: 2, z: 4, core: 2. Of those that a mesh axis runs over, the one named last changes fastest.
Arguments:
- wave: float32 [1313280], P(('dp', 'narrow')), may hold values from -6 to 6
- clip_ids: int32 [4096], P(('dp', 'narrow')), may hold values from 0 to 95, never falling along the last dimension, each value on 1 to 128 neighbouring positions
- span_starts: int32 [4096], P(('dp', 'narrow')), may hold values 0 or 1
- step_count: int32 [1], replicated, may hold values from 2 to 20
- conv_small: float32 [12, 512], replicated, as said below
- conv_stack: float32 [8192, 512], P(('dp', 'narrow')), may hold values from -0.25 to 0.25
- side: float32 [768, 2192], P('dp', 'narrow'), may hold values from -0.21875 to 0.21875
- vectors: float32 [10, 768], replicated, as said below
- block: float32 [3, 768, 3072], P(None, 'dp', 'narrow')
- teacher_block: float32 [3, 768, 3072], P(None, 'dp', 'narrow')
- teacher_vectors: float32 [10, 768], replicated, as said below
- small_mean: float32 [12, 512], replicated, may hold values from -4.4428212e-05 to 4.4428212e-05
- small_square: float32 [12, 512], replicated, may hold values from 1.2336662e-10 to 4.934665e-10
- stack_mean: float32 [8192, 512], P(('dp', 'narrow')), may hold values from -1.1107053e-05 to 1.1107053e-05
- stack_square: float32 [8192, 512], P(('dp', 'narrow')), may hold values from 7.710414e-12 to 3.0841656e-11
- side_mean: float32 [768, 2192], P('dp', 'narrow'), may hold values from -1.1107053e-05 to 1.1107053e-05
- side_square: float32 [768, 2192], P('dp', 'narrow'), may hold values from 7.710414e-12 to 3.0841656e-11
- vector_mean: float32 [10, 768], replicated, may hold values from -4.4428212e-05 to 4.4428212e-05
- vector_square: float32 [10, 768], replicated, may hold values from 1.2336662e-10 to 4.934665e-10
- block_momentum: float32 [3, 768, 3072], P(None, 'dp', 'narrow'), may hold values from -1.1107053e-05 to 1.1107053e-05
Outputs:
- loss: float32 [], replicated
- grad_norm: float32 [], replicated
- conv_small_next: float32 [12, 512], replicated
- small_mean_next: float32 [12, 512], replicated
- small_square_next: float32 [12, 512], replicated
- conv_stack_next: float32 [8192, 512], P(('dp', 'narrow'))
- stack_mean_next: float32 [8192, 512], P(('dp', 'narrow'))
- stack_square_next: float32 [8192, 512], P(('dp', 'narrow'))
- side_next: float32 [768, 2192], P('dp', 'narrow')
- side_mean_next: float32 [768, 2192], P('dp', 'narrow')
- side_square_next: float32 [768, 2192], P('dp', 'narrow')
- vectors_next: float32 [10, 768], replicated
- vector_mean_next: float32 [10, 768], replicated
- vector_square_next: float32 [10, 768], replicated
- block_next: float32 [3, 768, 3072], P(None, 'dp', 'narrow')
- momentum_next: float32 [3, 768, 3072], P(None, 'dp', 'narrow')
- teacher_block_next: float32 [3, 768, 3072], P(None, 'dp', 'narrow')
- teacher_vectors_next: float32 [10, 768], replicated
- block_copy: bfloat16 [3, 768, 3072], P(None, 'dp', 'narrow')
Inputs may be any that keep to these rules, and one draw needn't show every extreme that they name: `clip_ids`: clip numbers never fall along the frames; a clip has 1 to 128 frames, and some clip has exactly 128. `conv_small`: rows 10 are positive gains. `vectors`: rows 0, 2, 4 are positive gains. `teacher_vectors`: rows 0, 2, 4 are positive gains.
All inputs are finite; a program needn't handle non-finite values. No bound on the sum of `span_starts` on one device may be relied on, other than what follows from the above.
Results may differ from a plain program's by a relative error of at most 0.0025.
The roundings to bfloat16 on the way count: a program that leaves them out, or rounds other values in their place, can miss the bound.
Values may be sent and summed in bfloat16 or wider, within the bound.
No kernel may reach another device: no remote copies, remote signals or barrier semaphores. Data moves between devices by JAX's collectives and lax.ppermute only.
A program may use at most 448 MiB of HBM per device.

v0:
```python
import math
import jax
import jax.numpy as jnp
from jax import lax
from jax.sharding import PartitionSpec as P

D = 768
HEADS = 12
HEAD_DIM = 64
CH = 512
GROUPS = 16
POS_K = 19
SPAN = 10
EPS = 1e-05
VAR_FLOOR = 0.1
CLIP_LIMIT = 0.01
LR_ADAM = 0.03
LR_MUON = 2.0
DECAY = 0.5
WEIGHT_DECAY = 0.01
EMA_RATE = 0.5
KERNELS = (3, 3, 3, 3, 2, 2)
COEFF_A = 3.4445
COEFF_B = -4.775
COEFF_C = 2.0315
HIGHEST = lax.Precision.HIGHEST


def rounded(values):
    return lax.optimization_barrier(values.astype(jnp.bfloat16)).astype(jnp.float32)


def low(values):
    return values + lax.stop_gradient(rounded(values) - values)


def low_back(values):
    return rounded(values) + lax.stop_gradient(values - rounded(values))


def bprod(left_side, right_side):
    return low_back(jnp.einsum("bmk,bkn->bmn", left_side, right_side, precision=HIGHEST))


def matmul(left_side, right_side):
    return bprod(left_side[None], right_side[None])[0]


def layer_norm(values, gain, shift):
    center = values - jnp.mean(values, axis=-1, keepdims=True)
    spread = jnp.mean(center * center, axis=-1, keepdims=True)
    return center * lax.rsqrt(spread + EPS) * gain + shift


def strided_taps(values, kernel, stride, rows_out):
    return jnp.concatenate(
        [
            lax.slice_in_dim(values, offset, offset + stride * (rows_out - 1) + 1, stride, 0)
            for offset in range(kernel)
        ],
        axis=1,
    )


def encode(conv_small, conv_stack, side, vectors, wave):
    frames = (wave.shape[0] - 80) // 320
    length = 64 * frames + 15
    hidden = strided_taps(low(wave)[:, None], 10, 5, length)
    hidden = low(jax.nn.gelu(matmul(hidden, conv_small[:10]), approximate=False))
    row_offset = 0
    for kernel in KERNELS:
        length = (length - kernel) // 2 + 1
        tap_rows = strided_taps(hidden, kernel, 2, length)
        hidden = jax.nn.gelu(
            matmul(tap_rows, conv_stack[row_offset : row_offset + kernel * CH]), approximate=False
        )
        row_offset = row_offset + kernel * CH
        if row_offset < conv_stack.shape[0]:
            hidden = low(hidden)
    normed = low(layer_norm(hidden, conv_small[10], conv_small[11]))
    return matmul(normed, side[:, :CH].T) + vectors[6]


def neighbours(segment):
    frames = segment.shape[0]
    reach = POS_K // 2
    padded = jnp.pad(segment, (reach, reach), constant_values=-1)
    return jnp.stack(
        [padded[offset : offset + frames] == segment for offset in range(POS_K)], 0
    ).astype(jnp.float32)[:, :, None]


def masked_of(starts):
    frames = starts.shape[0]
    padded = jnp.pad(starts, (SPAN - 1, 0))
    return (
        jnp.max(jnp.stack([padded[offset : offset + frames] for offset in range(SPAN)], 0), axis=0)
        > 0
    )


def position(values, side, pos_bias, nearby):
    frames = values.shape[0]
    group_width = D // GROUPS
    reach = POS_K // 2
    padded = jnp.pad(low(values), ((reach, reach), (0, 0)))
    tap_rows = jnp.stack([padded[offset : offset + frames] for offset in range(POS_K)], 0) * nearby
    tap_rows = (
        tap_rows.reshape(POS_K, frames, GROUPS, group_width)
        .transpose(2, 1, 0, 3)
        .reshape(GROUPS, frames, POS_K * group_width)
    )
    kernel = side[:, CH : CH + POS_K * group_width].reshape(GROUPS, group_width, POS_K, group_width)
    kernel = kernel.transpose(0, 2, 1, 3).reshape(GROUPS, POS_K * group_width, group_width)
    mixed = bprod(tap_rows, kernel).transpose(1, 0, 2).reshape(frames, D)
    return jax.nn.gelu(mixed + pos_bias, approximate=False)


def transform(values, side, block, vectors, nearby, attend):
    frames = values.shape[0]
    hidden = layer_norm(values + position(values, side, vectors[7], nearby), vectors[0], vectors[1])
    triple = low(matmul(low(hidden), block[0][:, : 3 * D]))
    heads = triple.reshape(frames, 3, HEADS, HEAD_DIM).transpose(1, 2, 0, 3)
    scores = bprod(heads[0], heads[1].transpose(0, 2, 1)) / math.sqrt(HEAD_DIM)
    scores = jnp.where(attend[None], scores, -1e30)
    weights = low(jax.nn.softmax(scores, axis=-1))
    mixed = bprod(weights, heads[2]).transpose(1, 0, 2).reshape(frames, D)
    hidden = layer_norm(hidden + matmul(low(mixed), block[0][:, 3 * D :]), vectors[2], vectors[3])
    inner = low(jax.nn.gelu(matmul(low(hidden), block[1]), approximate=False))
    return layer_norm(hidden + matmul(inner, block[2].T), vectors[4], vectors[5])


def target_of(feats, side, teacher_block, teacher_vectors, nearby, attend):
    output = transform(feats, side, teacher_block, teacher_vectors, nearby, attend)
    member = attend.astype(jnp.float32)
    clip_size = jnp.sum(member, axis=1, keepdims=True)
    average = jnp.dot(member, output, precision=HIGHEST) / clip_size
    center = output - average
    spread = jnp.dot(member, center * center, precision=HIGHEST) / clip_size
    return center * lax.rsqrt(jnp.maximum(spread, VAR_FLOOR))


def student_loss(feats, side, block, vectors, nearby, attend, masked, target, total):
    chosen = masked[:, None]
    values = jnp.where(chosen, vectors[9], feats)
    hidden = transform(values, side, block, vectors, nearby, attend)
    predict = matmul(low(hidden), side[:, CH + POS_K * (D // GROUPS) :]) + vectors[8]
    error = jnp.where(chosen, predict - target, 0.0)
    return jnp.sum(error * error) / (total * math.sqrt(D))


def local_step(
    wave,
    segment,
    starts,
    conv_small,
    conv_stack,
    side,
    vectors,
    block,
    teacher_block,
    teacher_vectors,
    total,
):
    nearby = neighbours(segment)
    attend = segment[:, None] == segment[None, :]
    masked = masked_of(starts)
    feats, encode_back = jax.vjp(
        lambda small_part, stack_part, side_part, vector_part: encode(
            low(small_part), low(stack_part), low(side_part), low(vector_part), wave
        ),
        conv_small,
        conv_stack,
        side,
        vectors,
    )
    target = target_of(feats, low(side), low(teacher_block), low(teacher_vectors), nearby, attend)
    loss_part, student_back = jax.vjp(
        lambda feat_part, side_part, block_part, vector_part: student_loss(
            feat_part,
            low(side_part),
            low(block_part),
            low(vector_part),
            nearby,
            attend,
            masked,
            target,
            total,
        ),
        feats,
        side,
        block,
        vectors,
    )
    feat_grad, side_two, block_grad, vector_two = student_back(jnp.ones_like(loss_part))
    small_grad, stack_grad, side_one, vector_one = encode_back(feat_grad)
    return (
        loss_part,
        small_grad,
        stack_grad,
        side_one + side_two,
        block_grad,
        vector_one + vector_two,
    )


def adamw(weight, grad, first, second, power):
    first = DECAY * first + (1.0 - DECAY) * grad
    second = DECAY * second + (1.0 - DECAY) * grad * grad
    unbias = 1.0 - power
    step_size = first / unbias / (jnp.sqrt(second / unbias) + 1e-08)
    return (weight - LR_ADAM * (step_size + WEIGHT_DECAY * weight), first, second)


def orthogonal(matrix, gram_total):
    blocks = matrix
    for iteration in range(5):
        gram_matrix = gram_total(jnp.einsum("brc,bsc->brs", blocks, blocks, precision=HIGHEST))
        if iteration == 0:
            scales = 1.0 / (jnp.sqrt(jnp.trace(gram_matrix, axis1=1, axis2=2)) + 1e-07)
            blocks = blocks * scales[:, None, None]
            gram_matrix = gram_matrix * (scales * scales)[:, None, None]
        polynom = COEFF_B * gram_matrix + COEFF_C * jnp.einsum(
            "brs,bst->brt", gram_matrix, gram_matrix, precision=HIGHEST
        )
        blocks = COEFF_A * blocks + jnp.einsum("brs,bsc->brc", polynom, blocks, precision=HIGHEST)
    return blocks.reshape(matrix.shape)


def apply_updates(factor, power, weights, grads, states, gram_total):
    (
        small_weight,
        stack_weight,
        side_weight,
        vector_weight,
        block_weight,
        teacher_weight,
        teacher_vector,
    ) = weights
    small_grad, stack_grad, side_grad, block_grad, vector_grad = grads
    small_next = adamw(small_weight, factor * small_grad, states[0], states[1], power)
    stack_next = adamw(stack_weight, factor * stack_grad, states[2], states[3], power)
    side_next = adamw(side_weight, factor * side_grad, states[4], states[5], power)
    vector_next = adamw(vector_weight, factor * vector_grad, states[6], states[7], power)
    momentum = DECAY * states[8] + factor * block_grad
    block_next = block_weight * (1.0 - LR_MUON * WEIGHT_DECAY) - LR_MUON * orthogonal(
        momentum, gram_total
    )
    teacher_next = EMA_RATE * teacher_weight + (1.0 - EMA_RATE) * block_next
    teacher_vec_next = EMA_RATE * teacher_vector + (1.0 - EMA_RATE) * vector_next[0]
    return (
        small_next
        + stack_next
        + side_next
        + vector_next
        + (block_next, momentum, teacher_next, teacher_vec_next, block_next.astype(jnp.bfloat16))
    )


def narrow_total(gram_matrix):
    return lax.psum(gram_matrix, "narrow")


def per_device(
    wave,
    clip_ids,
    span_starts,
    step_count,
    conv_small,
    conv_stack,
    side,
    vectors,
    block,
    teacher_block,
    teacher_vectors,
    small_mean,
    small_square,
    stack_mean,
    stack_square,
    side_mean,
    side_square,
    vector_mean,
    vector_square,
    block_momentum,
):
    parts = (
        block.astype(jnp.bfloat16),
        teacher_block.astype(jnp.bfloat16),
        side.astype(jnp.bfloat16),
    )
    parts = (
        lax.all_gather(parts[0], "narrow", axis=2, tiled=True),
        lax.all_gather(parts[1], "narrow", axis=2, tiled=True),
        lax.all_gather(parts[2], "narrow", axis=1, tiled=True),
    )
    parts = (
        lax.all_gather(parts[0], "dp", axis=1, tiled=True),
        lax.all_gather(parts[1], "dp", axis=1, tiled=True),
        lax.all_gather(parts[2], "dp", axis=0, tiled=True),
    )
    whole_block = parts[0].astype(jnp.float32)
    whole_teacher = parts[1].astype(jnp.float32)
    whole_side = parts[2].astype(jnp.float32)
    whole_stack = lax.all_gather(
        conv_stack.astype(jnp.bfloat16), ("dp", "narrow"), axis=0, tiled=True
    ).astype(jnp.float32)
    masked_here = jnp.sum(masked_of(span_starts).astype(jnp.float32))
    total = jnp.maximum(lax.psum(masked_here, ("dp", "narrow")), 1.0)
    loss_part, small_grad, stack_grad, side_grad, block_grad, vector_grad = local_step(
        wave,
        clip_ids,
        span_starts,
        conv_small,
        whole_stack,
        whole_side,
        vectors,
        whole_block,
        whole_teacher,
        teacher_vectors,
        total,
    )
    row_parts = [
        lax.psum_scatter(block_grad[matrix_index], "dp", scatter_dimension=0, tiled=True)
        for matrix_index in range(3)
    ]
    side_rows = lax.psum_scatter(side_grad, "dp", scatter_dimension=0, tiled=True)
    pieces = (
        lax.psum_scatter(jnp.stack(row_parts, 0), "narrow", scatter_dimension=2, tiled=True),
        lax.psum_scatter(side_rows, "narrow", scatter_dimension=1, tiled=True),
    )
    block_piece = pieces[0]
    side_piece = pieces[1]
    stack_piece = lax.psum_scatter(stack_grad, ("dp", "narrow"), scatter_dimension=0, tiled=True)
    small_total, vector_total, loss_value = lax.psum(
        (small_grad, vector_grad, loss_part), ("dp", "narrow")
    )
    shard_squares = (
        jnp.sum(block_piece * block_piece)
        + jnp.sum(side_piece * side_piece)
        + jnp.sum(stack_piece * stack_piece)
    )
    grad_norm = jnp.sqrt(
        lax.psum(shard_squares, ("dp", "narrow"))
        + jnp.sum(small_total * small_total)
        + jnp.sum(vector_total * vector_total)
    )
    factor = jnp.minimum(1.0, CLIP_LIMIT / (grad_norm + 1e-06))
    power = jnp.power(DECAY, step_count[0].astype(jnp.float32))
    updates = apply_updates(
        factor,
        power,
        (conv_small, conv_stack, side, vectors, block, teacher_block, teacher_vectors),
        (small_total, stack_piece, side_piece, block_piece, vector_total),
        (
            small_mean,
            small_square,
            stack_mean,
            stack_square,
            side_mean,
            side_square,
            vector_mean,
            vector_square,
            block_momentum,
        ),
        narrow_total,
    )
    return (
        loss_value,
        grad_norm,
        updates[0],
        updates[1],
        updates[2],
        updates[3],
        updates[4],
        updates[5],
        updates[6],
        updates[7],
        updates[8],
        updates[9],
        updates[10],
        updates[11],
        updates[12],
        updates[13],
        updates[14],
        updates[15],
        updates[16],
    )


def solution(mesh):
    in_specs = (
        P(("dp", "narrow")),
        P(("dp", "narrow")),
        P(("dp", "narrow")),
        P(),
        P(),
        P(("dp", "narrow"), None),
        P("dp", "narrow"),
        P(),
        P(None, "dp", "narrow"),
        P(None, "dp", "narrow"),
        P(),
        P(),
        P(),
        P(("dp", "narrow"), None),
        P(("dp", "narrow"), None),
        P("dp", "narrow"),
        P("dp", "narrow"),
        P(),
        P(),
        P(None, "dp", "narrow"),
    )
    out_specs = (
        P(),
        P(),
        P(),
        P(),
        P(),
        P(("dp", "narrow"), None),
        P(("dp", "narrow"), None),
        P(("dp", "narrow"), None),
        P("dp", "narrow"),
        P("dp", "narrow"),
        P("dp", "narrow"),
        P(),
        P(),
        P(),
        P(None, "dp", "narrow"),
        P(None, "dp", "narrow"),
        P(None, "dp", "narrow"),
        P(),
        P(None, "dp", "narrow"),
    )
    return jax.shard_map(
        per_device, mesh=mesh, in_specs=in_specs, out_specs=out_specs, check_vma=False
    )
```

profile of v0, /device:TPU:0, one launch (start us, length us, event | category | flops | bytes accessed | tf_op | source)
XLA Modules:
  0.0 2137.3 jit_solution(9828727559107884883)
XLA Ops:
  34.9 39.8 %psum.70 = f32[]{:T(128)} all-reduce(f32[]{:T(128)} %get-tuple-element.160), channel_id=1, replica_groups=mesh['dp'=8,'narrow'=4] {'dp','narrow'}, use_global_device_ids=true, to_apply=%region_21.22 | all-reduce | flops 1 | bytes 8 | tf_op jit(solution)/shard_map/psum | solution.py:308
  100.9 13.5 fusion.404
  115.7 39.3 %fusion.62 = (bf16[8207,512]{1,0:T(8,128)(2,1)}, f32[8207,512]{1,0:T(8,128)}) fusion(f32[8207,512]{1,0:T(8,128)S(1)} %fusion.404, bf16[1,8207,512]{2,1,0:T(8,128)(2,1)S(1)} %convert_bitcast_fusion), kind=kLoop, calls=%fused_computation.104 | loop fusion | flops 285734912 | bytes 50423808 | tf_op jit(solution)/shard_map/jvp()/convert_element_type | solution.py:30
  155.0 17.5 subtract_add_fusion.2
  172.4 41.3 %slice.450 = f32[4103,512]{1,0:T(8,128)} slice(f32[8207,512]{1,0:T(8,128)} %subtract_add_fusion.2), slice={[0:8205:2], [0:512:1]} | slice | bytes 16805888 | tf_op jit(solution)/shard_map/jvp()/slice | solution.py:58
  213.7 41.2 %slice.451 = f32[4103,512]{1,0:T(8,128)} slice(f32[8207,512]{1,0:T(8,128)} %subtract_add_fusion.2), slice={[1:8206:2], [0:512:1]} | slice | bytes 16805888 | tf_op jit(solution)/shard_map/jvp()/slice | solution.py:58
  254.9 41.7 %slice.452 = f32[4103,512]{1,0:T(8,128)} slice(f32[8207,512]{1,0:T(8,128)} %subtract_add_fusion.2), slice={[2:8207:2], [0:512:1]} | slice | bytes 16805888 | tf_op jit(solution)/shard_map/jvp()/slice | solution.py:58
  337.2 14.6 subtract_add_fusion.4
  351.8 45.2 %fusion.4 = f32[4103,512]{1,0:T(8,128)S(1)} fusion(f32[4103,512]{1,0:T(8,128)} %slice.452, f32[4103,512]{1,0:T(8,128)} %slice.451, f32[4103,512]{1,0:T(8,128)} %slice.450, f32[8192,512]{1,0:T(8,128)} %subtract_add_fusion.4), kind=kOutput, calls=%fused_computation.11 | convolution fusion | flops 38733369344 | bytes 36763648 | tf_op jit(solution)/shard_map/jvp(bmk,bkn->bmn)/dot_general | solution.py:42
  397.6 20.1 fusion.95
  427.5 21.1 slice.454
  448.6 21.0 slice.455
  469.7 21.5 %slice.456 = f32[2051,512]{1,0:T(8,128)} slice(f32[4103,512]{1,0:T(8,128)} %subtract_add_fusion.5), slice={[2:4103:2], [0:512:1]} | slice | bytes 8400896 | tf_op jit(solution)/shard_map/jvp()/slice | solution.py:58
  491.2 24.3 %fusion.28 = f32[2051,512]{1,0:T(8,128)S(1)} fusion(f32[2051,512]{1,0:T(8,128)} %slice.456, f32[2051,512]{1,0:T(8,128)} %slice.455, f32[2051,512]{1,0:T(8,128)} %slice.454, f32[8192,512]{1,0:T(8,128)} %subtract_add_fusion.4), kind=kOutput, calls=%fused_computation.59 | convolution fusion | flops 19361964032 | bytes 19978240 | tf_op jit(solution)/shard_map/jvp(bmk,bkn->bmn)/dot_general | solution.py:42
  563.8 13.5 fusion.64
  604.3 19.5 slice.466
  623.8 19.9 slice.467
  767.5 22.5 %subtract_add_fusion = f32[3,768,3072]{2,1,0:T(8,128)} fusion(bf16[3,768,3072]{2,1,0:T(8,128)(2,1)} %all-gather.18.cloned.1.call-done), kind=kLoop, calls=%fused_computation.2 | loop fusion | flops 28311552 | bytes 42467328 | tf_op jit(solution)/shard_map/add | solution.py:34
  824.3 11.8 fusion.25
  836.9 22.6 %subtract_add_fusion.1 = f32[3,768,3072]{2,1,0:T(8,128)} fusion(bf16[3,768,3072]{2,1,0:T(8,128)(2,1)} %all-gather.14.cloned.1.call-done), kind=kLoop, calls=%fused_computation.3 | loop fusion | flops 28311552 | bytes 42467328 | tf_op jit(solution)/shard_map/jvp()/add | solution.py:34
  890.8 12.8 fusion.32
  962.6 21.4 %pad_add_fusion = f32[3,768,3072]{2,1,0:T(8,128)} fusion(f32[1,768,3072]{2,1,0:T(8,128)} %pad_bitcast_fusion, f32[1,768,3072]{2,1,0:T(8,128)} %pad_bitcast_fusion.1, f32[1,768,3072]{2,1,0:T(8,128)} %convolution_bitcast_fusion.1, f32[1,768,3072]{2,1,0:T(8,128)S(1)} %convolution_bitcast_fusion.2), kind=kLoop, calls=%fused_computation.4 | loop fusion | flops 21233664 | bytes 66060288 | tf_op jit(solution)/shard_map/transpose(jvp())/add_any | solution.py:122
  984.0 19.8 slice_bitcast_fusion.2
  1096.6 22.2 %pad.260 = f32[512,512]{0,1:T(8,128)} pad(f32[256,512]{0,1:T(8,128)} %get-tuple-element.231, f32[]{:T(128)} %constant.65.clone.1), padding=1_0_1x0_0_0 | pad | bytes 1572868 | tf_op jit(solution)/shard_map/transpose(jvp())/pad | solution.py:58
  1118.8 20.0 pad.261
  1190.2 16.7 pad.267
  1215.9 16.9 pad.269
  1242.6 14.2 fusion.103
  1266.7 32.8 %pad.271 = f32[4103,512]{1,0:T(8,128)} pad(f32[2051,512]{1,0:T(8,128)} %get-tuple-element.204, f32[]{:T(128)} %constant.65.clone.1), padding=2_0_1x0_0_0 | pad | bytes 12603396 | tf_op jit(solution)/shard_map/transpose(jvp())/pad | solution.py:58
  1299.5 32.6 %pad.272 = f32[4103,512]{1,0:T(8,128)} pad(f32[2051,512]{1,0:T(8,128)} %get-tuple-element.202, f32[]{:T(128)} %constant.65.clone.1), padding=1_1_1x0_0_0 | pad | bytes 12603396 | tf_op jit(solution)/shard_map/transpose(jvp())/pad | solution.py:58
  1332.1 32.6 %pad.273 = f32[4103,512]{1,0:T(8,128)} pad(f32[2051,512]{1,0:T(8,128)} %get-tuple-element.203, f32[]{:T(128)} %constant.65.clone.1), padding=0_2_1x0_0_0 | pad | bytes 12603396 | tf_op jit(solution)/shard_map/transpose(jvp())/pad | solution.py:58
  1364.7 135.9 %reduce-scatter.15.cloned.1.call-done = f32[96,3072]{1,0:T(8,128)} async-done(((f32[768,3072]{1,0:T(8,128)}), f32[96,3072]{1,0:T(8,128)}) %reduce-scatter.15.cloned.1.call-update) | async-done | bytes 1179664 | tf_op jit(solution)/shard_map/reduce_scatter | solution.py:323
  1504.9 19.7 fusion.88
  1540.1 16.8 fusion.90
  1557.0 26.4 %fusion.91 = f32[1536,512]{1,0:T(8,128)} fusion(f32[4103,512]{1,0:T(8,128)} %slice.452, f32[4103,512]{1,0:T(8,128)S(1)} %bitcast.1359, f32[4103,512]{1,0:T(8,128)S(1)} %bitcast.1357, bf16[1,4103,512]{2,1,0:T(8,128)(2,1)S(1)} %bitcast.1368), kind=kOutput, calls=%fused_computation.150 | convolution fusion | flops 38733369344 | bytes 32556032 | tf_op jit(solution)/shard_map/transpose(jvp(bmk,bkn->bmn))/dot_general | solution.py:42
  1596.8 25.8 %fusion.85 = f32[4103,1536]{1,0:T(8,128)} fusion(bf16[1,4103,512]{2,1,0:T(8,128)(2,1)} %fusion.88, f32[8192,512]{1,0:T(8,128)} %subtract_add_fusion.4), kind=kOutput, calls=%fused_computation.141 | convolution fusion | flops 38720765952 | bytes 32557056 | tf_op jit(solution)/shard_map/transpose(jvp(bmk,bkn->bmn))/dot_general | solution.py:42
  1622.6 17.9 fusion.480
  1640.4 65.6 %pad.277 = f32[8207,512]{1,0:T(8,128)} pad(f32[4103,512]{1,0:T(8,128)} %get-tuple-element.201, f32[]{:T(128)} %constant.65.clone.1), padding=2_0_1x0_0_0 | pad | bytes 25210884 | tf_op jit(solution)/shard_map/transpose(jvp())/pad | solution.py:58
  1706.0 64.6 %pad.278 = f32[8207,512]{1,0:T(8,128)} pad(f32[4103,512]{1,0:T(8,128)} %get-tuple-element.199, f32[]{:T(128)} %constant.65.clone.1), padding=1_1_1x0_0_0 | pad | bytes 25210884 | tf_op jit(solution)/shard_map/transpose(jvp())/pad | solution.py:58
  1770.6 64.4 %pad.279 = f32[8207,512]{1,0:T(8,128)} pad(f32[4103,512]{1,0:T(8,128)} %get-tuple-element.200, f32[]{:T(128)} %constant.65.clone.1), padding=0_2_1x0_0_0 | pad | bytes 25210884 | tf_op jit(solution)/shard_map/transpose(jvp())/pad | solution.py:58
  1835.0 34.4 %fusion.55 = bf16[1,8207,512]{2,1,0:T(8,128)(2,1)} fusion(f32[8207,512]{1,0:T(8,128)} %get-tuple-element.195, f32[8207,512]{1,0:T(8,128)} %pad.279, f32[8207,512]{1,0:T(8,128)} %pad.277, f32[8207,512]{1,0:T(8,128)} %pad.278, f32[8207,512]{1,0:T(8,128)} %copy-done, bf16[1,8207,512]{2,1,0:T(8,128)(2,1)} %copy-done.2), kind=kLoop, calls=%fused_computation.94 | loop fusion | flops 79837696 | bytes 100847616 | tf_op jit(solution)/shard_map/transpose(jvp())/convert_element_type | solution.py:30
  1877.0 15.1 fusion
  1901.4 43.9 %all-reduce.72 = (f32[]{:T(128)}, f32[]{:T(128)}, f32[12,512]{1,0:T(8,128)S(1)}, f32[10,768]{1,0:T(8,128)S(1)}) all-reduce(f32[]{:T(128)S(6)} %div.229, f32[]{:T(128)S(6)} %add.761, f32[12,512]{1,0:T(8,128)S(1)} %pad_add_fusion.9, f32[10,768]{1,0:T(8,128)S(1)} %add_add_fusion.5), channel_id=1, replica_groups=mesh['dp'=8,'narrow'=4] {'dp','narrow'}, use_global_device_ids=true, to_apply=%region_22.23 | all-reduce | flops 13826 | bytes 110608 | tf_op jit(solution)/shard_map/psum | solution.py:334
  1956.4 26.0 %all-reduce.79.cloned.1.call-done = f32[3,96,96]{2,1,0:T(8,128)} async-done(((f32[3,96,96]{2,1,0:T(8,128)}), f32[3,96,96]{2,1,0:T(8,128)}) %all-reduce.79.cloned.1.call-update) | async-done | bytes 110608 | tf_op jit(solution)/shard_map/psum | solution.py:261
  1990.1 29.0 %all-reduce.81.cloned.1.call-done = f32[3,96,96]{2,1,0:T(8,128)} async-done(((f32[3,96,96]{2,1,0:T(8,128)}), f32[3,96,96]{2,1,0:T(8,128)}) %all-reduce.81.cloned.1.call-update) | async-done | bytes 110608 | tf_op jit(solution)/shard_map/psum | solution.py:261
  2024.0 30.5 %all-reduce.83.cloned.1.call-done = f32[3,96,96]{2,1,0:T(8,128)} async-done(((f32[3,96,96]{2,1,0:T(8,128)}), f32[3,96,96]{2,1,0:T(8,128)}) %all-reduce.83.cloned.1.call-update) | async-done | bytes 110608 | tf_op jit(solution)/shard_map/psum | solution.py:261
  2060.1 30.0 %all-reduce.85.cloned.1.call-done = f32[3,96,96]{2,1,0:T(8,128)} async-done(((f32[3,96,96]{2,1,0:T(8,128)}), f32[3,96,96]{2,1,0:T(8,128)}) %all-reduce.85.cloned.1.call-update) | async-done | bytes 110608 | tf_op jit(solution)/shard_map/psum | solution.py:261
  2100.8 24.8 %all-reduce.87.cloned.1.call-done = f32[3,96,96]{2,1,0:T(8,128)} async-done(((f32[3,96,96]{2,1,0:T(8,128)}), f32[3,96,96]{2,1,0:T(8,128)}) %all-reduce.87.cloned.1.call-update) | async-done | bytes 110608 | tf_op jit(solution)/shard_map/psum | solution.py:261
  (921 shorter events, 685.8 us)
Async XLA Ops:
  7.2 26.5 %all-gather.16.cloned.1.call-start = ((), (), s32[]{:S(2)}) async-start(), calls=%async_computation.10 | async-start | bytes 2211840 | tf_op jit(solution)/shard_map/all_gather | solution.py:293
  9.3 65.5 %copy-start.135 = (f32[41040]{0:T(1024)S(1)}, f32[41040]{0:T(1024)}, u32[]{:S(2)}) copy-start(f32[41040]{0:T(1024)} %param.20) | copy-start | bytes 492484
  9.3 292.0 %all-gather.12.cloned.1.call-start = ((), (), s32[]{:S(2)}) async-start(), calls=%async_computation.8 | async-start | bytes 2211840 | tf_op jit(solution)/shard_map/all_gather | solution.py:292
  11.4 86.8 %copy-start.140 = (f32[12,512]{1,0:T(8,128)S(1)}, f32[12,512]{1,0:T(8,128)}, u32[]{:S(2)}) copy-start(f32[12,512]{1,0:T(8,128)} %param.24) | copy-start | bytes 73732
  11.4 290.0 %all-gather.10.cloned.1.call-start = ((), (), s32[]{:S(2)}) async-start(), calls=%async_computation.7 | async-start | bytes 3981312 | tf_op jit(solution)/shard_map/all_gather | solution.py:299
  22.3 314.9 %all-gather.8.cloned.1.call-start = ((), (), s32[]{:S(2)}) async-start(), calls=%async_computation.6 | async-start | bytes 8650752 | tf_op jit(solution)/shard_map/all_gather | solution.py:304
  23.1 744.4 %all-gather.18.cloned.1.call-start = ((), (), s32[]{:S(2)}) async-start(), calls=%async_computation.11 | async-start | bytes 15925248 | tf_op jit(solution)/shard_map/all_gather | solution.py:298
  33.7 803.2 %all-gather.14.cloned.1.call-start = ((), (), s32[]{:S(2)}) async-start(), calls=%async_computation.9 | async-start | bytes 15925248 | tf_op jit(solution)/shard_map/all_gather | solution.py:297
  114.4 40.6 %copy-start = (f32[8207,512]{1,0:T(8,128)}, f32[8207,512]{1,0:T(8,128)S(1)}, u32[]{:S(2)}) copy-start(f32[8207,512]{1,0:T(8,128)S(1)} %fusion.404) | copy-start | bytes 50423812
  115.6 39.3 %copy-start.2 = (bf16[1,8207,512]{2,1,0:T(8,128)(2,1)}, bf16[1,8207,512]{2,1,0:T(8,128)(2,1)S(1)}, u32[]{:S(2)}) copy-start(bf16[1,8207,512]{2,1,0:T(8,128)(2,1)S(1)} %convert_bitcast_fusion) | copy-start | bytes 25211908
  254.9 41.7 %copy-start.136 = (f32[10,768]{1,0:T(8,128)S(1)}, f32[10,768]{1,0:T(8,128)}, u32[]{:S(2)}) copy-start(f32[10,768]{1,0:T(8,128)} %param.27) | copy-start | bytes 92164
  254.9 41.7 %copy-start.216 = (s32[128]{0:T(128)S(1)}, s32[128]{0:T(128)}, u32[]{:S(2)}) copy-start(s32[128]{0:T(128)} %param.21) | copy-start | bytes 1540
  254.9 42.6 %copy-start.137 = (f32[10,768]{1,0:T(8,128)S(1)}, f32[10,768]{1,0:T(8,128)}, u32[]{:S(2)}) copy-start(f32[10,768]{1,0:T(8,128)} %param.30) | copy-start | bytes 92164
  301.4 1063.4 %reduce-scatter.11.cloned.1.call-start = ((), (), s32[]{:S(2)}) async-start(), calls=%async_computation.12 | async-start | bytes 10616832 | tf_op jit(solution)/shard_map/reduce_scatter | solution.py:323
  659.2 42.9 %copy-start.32 = (f32[128,768]{1,0:T(8,128)}, f32[128,768]{1,0:T(8,128)S(1)}, u32[]{:S(2)}) copy-start(f32[128,768]{1,0:T(8,128)S(1)} %get-tuple-element.175) | copy-start | bytes 1179652
  767.1 96.8 %copy-start.179 = (f32[128]{0:T(128)}, f32[128]{0:T(128)S(1)}, u32[]{:S(2)}) copy-start(f32[128]{0:T(128)S(1)} %broadcast_multiply_fusion.6) | copy-start | bytes 1540
  767.3 96.6 %copy-start.190 = (f32[128]{0:T(128)}, f32[128]{0:T(128)S(1)}, u32[]{:S(2)}) copy-start(f32[128]{0:T(128)S(1)} %fusion.431) | copy-start | bytes 1540
  767.5 96.5 %copy-start.90 = (bf16[128,768]{1,0:T(8,128)(2,1)}, bf16[128,768]{1,0:T(8,128)(2,1)S(1)}, u32[]{:S(2)}) copy-start(bf16[128,768]{1,0:T(8,128)(2,1)S(1)} %fusion.441) | copy-start | bytes 589828
  877.4 38.1 %slice-start = ((s8[28311552]{0:T(1024)(128)(4,1)}), s8[4194304]{0:T(1024)(128)(4,1)S(1)}, s32[]{:S(2)}) async-start(s8[28311552]{0:T(1024)(128)(4,1)} %bitcast.1344), calls=%async_computation.23 | async-start | bytes 8388608
  878.1 37.4 %slice-start.1 = ((s8[28311552]{0:T(1024)(128)(4,1)}), s8[4194304]{0:T(1024)(128)(4,1)S(1)}, s32[]{:S(2)}) async-start(s8[28311552]{0:T(1024)(128)(4,1)} %bitcast.1344), calls=%async_computation.24 | async-start | bytes 8388608
  887.0 28.5 %slice-start.2 = ((s8[28311552]{0:T(1024)(128)(4,1)}), s8[4194304]{0:T(1024)(128)(4,1)S(1)}, s32[]{:S(2)}) async-start(s8[28311552]{0:T(1024)(128)(4,1)} %bitcast.1344), calls=%async_computation.25 | async-start | bytes 8388608
  1003.8 360.9 %reduce-scatter.13.cloned.1.call-start = ((), (), s32[]{:S(2)}) async-start(), calls=%async_computation.13 | async-start | bytes 10616832 | tf_op jit(solution)/shard_map/reduce_scatter | solution.py:323
  1004.6 496.0 %reduce-scatter.15.cloned.1.call-start = ((), (), s32[]{:S(2)}) async-start(), calls=%async_computation.14 | async-start | bytes 10616832 | tf_op jit(solution)/shard_map/reduce_scatter | solution.py:323
  1005.3 870.0 %reduce-scatter.21.cloned.1.call-start = ((), (), s32[]{:S(2)}) async-start(), calls=%async_computation.22 | async-start | bytes 7962624
  1084.6 811.0 %reduce-scatter.17.cloned.1.call-start = ((), (), s32[]{:S(2)}) async-start(), calls=%async_computation.15 | async-start | bytes 4423680 | tf_op jit(solution)/shard_map/reduce_scatter | solution.py:328
  1092.9 45.9 %copy-start.19 = (f32[512,512]{0,1:T(8,128)S(1)}, f32[512,512]{0,1:T(8,128)}, u32[]{:S(2)}) copy-start(f32[512,512]{0,1:T(8,128)} %copy-done.18) | copy-start | bytes 3145732
  1092.9 45.9 %copy-start.36 = (f32[512,512]{0,1:T(8,128)S(1)}, f32[512,512]{0,1:T(8,128)}, u32[]{:S(2)}) copy-start(f32[512,512]{0,1:T(8,128)} %copy-done.35) | copy-start | bytes 3145732
  1092.9 45.9 %copy-start.44 = (bf16[1,512,512]{1,2,0:T(8,128)(2,1)S(1)}, bf16[1,512,512]{1,2,0:T(8,128)(2,1)}, u32[]{:S(2)}) copy-start(bf16[1,512,512]{1,2,0:T(8,128)(2,1)} %copy-done.43) | copy-start | bytes 1572868
  1148.3 26.4 %copy-start.15 = (f32[1025,512]{1,0:T(8,128)S(1)}, f32[1025,512]{1,0:T(8,128)}, u32[]{:S(2)}) copy-start(f32[1025,512]{1,0:T(8,128)} %copy-done.14) | copy-start | bytes 6297604
  1148.3 26.4 %copy-start.24 = (bf16[1,1025,512]{2,1,0:T(8,128)(2,1)S(1)}, bf16[1,1025,512]{2,1,0:T(8,128)(2,1)}, u32[]{:S(2)}) copy-start(bf16[1,1025,512]{2,1,0:T(8,128)(2,1)} %copy-done.23) | copy-start | bytes 3148804
  1504.8 394.2 %reduce-scatter.19.cloned.1.call-start = ((), (), s32[]{:S(2)}) async-start(), calls=%async_computation.16 | async-start | bytes 17301504 | tf_op jit(solution)/shard_map/reduce_scatter | solution.py:333
  1594.1 388.3 %all-reduce.79.cloned.1.call-start = ((), (), s32[]{:S(2)}) async-start(), calls=%async_computation.17 | async-start | bytes 294912 | tf_op jit(solution)/shard_map/psum | solution.py:261
  1835.0 34.5 %copy-start.49 = (f32[8207,10]{0,1:T(8,128)S(1)}, f32[8207,10]{0,1:T(8,128)}, u32[]{:S(2)}) copy-start(f32[8207,10]{0,1:T(8,128)} %copy-done.48) | copy-start | bytes 984844
  1875.3 73.3 %copy-start.130 = (f32[3,96,768]{2,1,0:T(8,128)S(1)}, f32[3,96,768]{2,1,0:T(8,128)}, u32[]{:S(2)}) copy-start(f32[3,96,768]{2,1,0:T(8,128)} %param.39) | copy-start | bytes 2654212
  1877.0 74.9 %copy-start.129 = (f32[96,548]{1,0:T(8,128)S(1)}, f32[96,548]{1,0:T(8,128)}, u32[]{:S(2)}) copy-start(f32[96,548]{1,0:T(8,128)} %param.26) | copy-start | bytes 631300
  1892.1 2.2 collective-permute-start
  1945.4 39.5 %copy-start.148 = (f32[10,768]{1,0:T(8,128)}, f32[10,768]{1,0:T(8,128)S(1)}, u32[]{:S(2)}) copy-start(f32[10,768]{1,0:T(8,128)S(1)} %get-tuple-element.134) | copy-start | bytes 92164
  1949.9 40.2 %copy-start.29 = (f32[3,96,768]{2,1,0:T(8,128)}, f32[3,96,768]{2,1,0:T(8,128)S(1)}, u32[]{:S(2)}) copy-start(f32[3,96,768]{2,1,0:T(8,128)S(1)} %multiply_add_fusion) | copy-start | bytes 2654212
  1949.9 37.5 %copy-start.85 = (f32[256,512]{1,0:T(8,128)S(1)}, f32[256,512]{1,0:T(8,128)}, u32[]{:S(2)}) copy-start(f32[256,512]{1,0:T(8,128)} %param.25) | copy-start | bytes 1572868
  1950.0 37.5 %copy-start.86 = (f32[256,512]{1,0:T(8,128)S(1)}, f32[256,512]{1,0:T(8,128)}, u32[]{:S(2)}) copy-start(f32[256,512]{1,0:T(8,128)} %reduce-scatter.19.cloned.1.call-done) | copy-start | bytes 1572868
  1951.6 67.6 %all-reduce.81.cloned.1.call-start = ((), (), s32[]{:S(2)}) async-start(), calls=%async_computation.18 | async-start | bytes 294912 | tf_op jit(solution)/shard_map/psum | solution.py:261
  1987.4 67.2 %all-reduce.83.cloned.1.call-start = ((), (), s32[]{:S(2)}) async-start(), calls=%async_computation.19 | async-start | bytes 294912 | tf_op jit(solution)/shard_map/psum | solution.py:261
  1990.1 32.9 %copy-start.126 = (f32[96,548]{0,1:T(8,128)S(1)}, f32[96,548]{0,1:T(8,128)}, u32[]{:S(2)}) copy-start(f32[96,548]{0,1:T(8,128)} %copy.284) | copy-start | bytes 631300
  1990.1 32.9 %copy-start.127 = (f32[96,548]{0,1:T(8,128)S(1)}, f32[96,548]{0,1:T(8,128)}, u32[]{:S(2)}) copy-start(f32[96,548]{0,1:T(8,128)} %copy.285) | copy-start | bytes 631300
  2022.9 67.2 %all-reduce.85.cloned.1.call-start = ((), (), s32[]{:S(2)}) async-start(), calls=%async_computation.20 | async-start | bytes 294912 | tf_op jit(solution)/shard_map/psum | solution.py:261
  2056.8 70.1 %copy-start.66 = (f32[3,96,768]{2,1,0:T(8,128)S(1)}, f32[3,96,768]{2,1,0:T(8,128)}, u32[]{:S(2)}) copy-start(f32[3,96,768]{2,1,0:T(8,128)} %param.29) | copy-start | bytes 2654212
  2056.8 70.1 %copy-start.67 = (f32[3,96,768]{2,1,0:T(8,128)S(1)}, f32[3,96,768]{2,1,0:T(8,128)}, u32[]{:S(2)}) copy-start(f32[3,96,768]{2,1,0:T(8,128)} %param.28) | copy-start | bytes 2654212
  2058.4 67.1 %all-reduce.87.cloned.1.call-start = ((), (), s32[]{:S(2)}) async-start(), calls=%async_computation.21 | async-start | bytes 294912 | tf_op jit(solution)/shard_map/psum | solution.py:261
  (221 other events, 1642.6 us)
Sparse Core Ops, SparseCore 0:
  10.2 23.4 all-gather.15
  35.8 20.9 all-gather.11
  59.5 65.1 all-gather.9
  128.0 76.0 all-gather.7
  206.2 194.1 all-gather.17
  402.4 193.7 all-gather.13
  1003.9 164.3 reduce-scatter.10
  1171.9 162.3 reduce-scatter.12
  1338.0 162.5 reduce-scatter.14
  1504.1 128.1 reduce-scatter.20
  1635.0 39.4 reduce-scatter.16
  1676.7 182.9 reduce-scatter.18
  1951.7 30.6 all-reduce.78
  1987.5 31.5 all-reduce.80
  2023.0 31.5 all-reduce.82
  2058.5 31.5 all-reduce.84
  2094.0 31.5 all-reduce.86
where the time goes:
time: 2160 us; the launch traced here: 2140 us
  local copies, waits for them, and re-layouts  972 us (45%)
  matrix products  397 us (18%)
  other arithmetic  342 us (16%)
  waiting for transfers between devices  289 us (13%)
  blocking collectives  107 us (5%)
  between operations  27.1 us (1%)
    pad x16, local copies, waits for them, and re-layouts, strided_taps(): lax.slice_in_dim(values, offset, offset + stride * (rows_out - 1) + 1, st...  404 us
    dot_general x54, matrix products, bprod(): jnp.einsum('bmk,bkn->bmn', left_side, right_side, precision=HIGHEST)  376 us
    slice x26, local copies, waits for them, and re-layouts, strided_taps(): lax.slice_in_dim(values, offset, offset + stride * (rows_out - 1) + 1, st...  293 us
    psum x5, waiting for transfers between devices, narrow_total(): return lax.psum(gram_matrix, 'narrow')  140 us
    reduce_scatter x3, waiting for transfers between devices, per_device(): lax.psum_scatter(block_grad[matrix_index], 'dp', scatter_dimension=0, til...  136 us
    add x18, other arithmetic, low(): return values + lax.stop_gradient(rounded(values) - values)  94 us
    convert_element_type x43, other arithmetic, rounded(): values.astype(jnp.bfloat16)  91.3 us
    convert_element_type x13, other arithmetic, rounded(): lax.optimization_barrier(values.astype(jnp.bfloat16)).astype(jnp.float32)  72.3 us
  transfers between devices with their start and end apart: 18, of which 8 were waited for; matrix products, arithmetic and copies ran while one was open for 71% of the time, Pallas kernels for 0%

commit v1 on v0

--- a/solution.py
+++ b/solution.py
@@ -258,7 +258,7 @@
 
 
 def narrow_total(gram_matrix):
-    return lax.psum(gram_matrix, "narrow")
+    return jnp.sum(lax.all_gather(gram_matrix, "narrow"), axis=0)
 
 
 def per_device(

time: 2160 us -> 2050 us (0.949)
  waiting for transfers between devices: 289 us -> 148 us
  blocking collectives: 107 us -> 148 us
    psum x5 -> x0, waiting for transfers between devices: 140 us -> none  [narrow_total(): return lax.psum(gram_matrix, 'narrow')]
    all_gather x0 -> x5, blocking collectives: none -> 40 us  [narrow_total(): return jnp.sum(lax.all_gather(gram_matrix, 'narrow'), axis=0)]
    unnamed x548 -> x556, local copies, waits for them, and re-layouts: 58.9 us -> 55.1 us
  transfers between devices with their start and end apart: 18 -> 13, of which waited for: 8 -> 3; matrix products, arithmetic and copies ran while one was open for 71% -> 74% of each run, Pallas kernels for 0% -> 0%
where the time goes in v1:
time: 2050 us; the launch traced here: 2020 us
  local copies, waits for them, and re-layouts  968 us (47%)
  matrix products  389 us (19%)
  other arithmetic  342 us (17%)
  waiting for transfers between devices  148 us (7%)
  blocking collectives  148 us (7%)
  between operations  27.4 us (1%)
    pad x16, local copies, waits for them, and re-layouts, strided_taps(): lax.slice_in_dim(values, offset, offset + stride * (rows_out - 1) + 1, st...  403 us
    dot_general x54, matrix products, bprod(): jnp.einsum('bmk,bkn->bmn', left_side, right_side, precision=HIGHEST)  376 us
    slice x26, local copies, waits for them, and re-layouts, strided_taps(): lax.slice_in_dim(values, offset, offset + stride * (rows_out - 1) + 1, st...  293 us
    reduce_scatter x3, waiting for transfers between devices, per_device(): lax.psum_scatter(block_grad[matrix_index], 'dp', scatter_dimension=0, til...  136 us
    add x18, other arithmetic, low(): return values + lax.stop_gradient(rounded(values) - values)  94 us
    convert_element_type x43, other arithmetic, rounded(): values.astype(jnp.bfloat16)  91.3 us
    convert_element_type x13, other arithmetic, rounded(): lax.optimization_barrier(values.astype(jnp.bfloat16)).astype(jnp.float32)  72.2 us
    slice x38, local copies, waits for them, and re-layouts, position(): padded[offset:offset + frames]  65.7 us
  transfers between devices with their start and end apart: 13, of which 3 were waited for; matrix products, arithmetic and copies ran while one was open for 74% of the time, Pallas kernels for 0%

profile of v1, /device:TPU:0, one launch (start us, length us, event | category | flops | bytes accessed | tf_op | source)
XLA Modules:
  0.0 2024.1 jit_solution(12906304272802182615)
XLA Ops:
  34.9 39.8 %psum.35 = f32[]{:T(128)} all-reduce(f32[]{:T(128)} %get-tuple-element.160), channel_id=1, replica_groups=mesh['dp'=8,'narrow'=4] {'dp','narrow'}, use_global_device_ids=true, to_apply=%region_21.22 | all-reduce | flops 1 | bytes 8 | tf_op jit(solution)/shard_map/psum | solution.py:308
  101.0 13.5 fusion.404
  115.7 39.3 %fusion.62 = (bf16[8207,512]{1,0:T(8,128)(2,1)}, f32[8207,512]{1,0:T(8,128)}) fusion(f32[8207,512]{1,0:T(8,128)S(1)} %fusion.404, bf16[1,8207,512]{2,1,0:T(8,128)(2,1)S(1)} %convert_bitcast_fusion), kind=kLoop, calls=%fused_computation.104 | loop fusion | flops 285734912 | bytes 50423808 | tf_op jit(solution)/shard_map/jvp()/convert_element_type | solution.py:30
  155.0 17.4 subtract_add_fusion.2
  172.5 41.3 %slice.450 = f32[4103,512]{1,0:T(8,128)} slice(f32[8207,512]{1,0:T(8,128)} %subtract_add_fusion.2), slice={[0:8205:2], [0:512:1]} | slice | bytes 16805888 | tf_op jit(solution)/shard_map/jvp()/slice | solution.py:58
  213.8 41.1 %slice.451 = f32[4103,512]{1,0:T(8,128)} slice(f32[8207,512]{1,0:T(8,128)} %subtract_add_fusion.2), slice={[1:8206:2], [0:512:1]} | slice | bytes 16805888 | tf_op jit(solution)/shard_map/jvp()/slice | solution.py:58
  254.9 41.8 %slice.452 = f32[4103,512]{1,0:T(8,128)} slice(f32[8207,512]{1,0:T(8,128)} %subtract_add_fusion.2), slice={[2:8207:2], [0:512:1]} | slice | bytes 16805888 | tf_op jit(solution)/shard_map/jvp()/slice | solution.py:58
  318.7 11.1 copy.239
  337.3 14.6 subtract_add_fusion.4
  351.9 45.2 %fusion.4 = f32[4103,512]{1,0:T(8,128)S(1)} fusion(f32[4103,512]{1,0:T(8,128)} %slice.452, f32[4103,512]{1,0:T(8,128)} %slice.451, f32[4103,512]{1,0:T(8,128)} %slice.450, f32[8192,512]{1,0:T(8,128)} %subtract_add_fusion.4), kind=kOutput, calls=%fused_computation.11 | convolution fusion | flops 38733369344 | bytes 36763648 | tf_op jit(solution)/shard_map/jvp(bmk,bkn->bmn)/dot_general | solution.py:42
  397.7 20.1 fusion.95
  427.7 21.0 %slice.454 = f32[2051,512]{1,0:T(8,128)} slice(f32[4103,512]{1,0:T(8,128)} %subtract_add_fusion.5), slice={[0:4101:2], [0:512:1]} | slice | bytes 8400896 | tf_op jit(solution)/shard_map/jvp()/slice | solution.py:58
  448.7 21.0 %slice.455 = f32[2051,512]{1,0:T(8,128)} slice(f32[4103,512]{1,0:T(8,128)} %subtract_add_fusion.5), slice={[1:4102:2], [0:512:1]} | slice | bytes 8400896 | tf_op jit(solution)/shard_map/jvp()/slice | solution.py:58
  469.7 21.5 %slice.456 = f32[2051,512]{1,0:T(8,128)} slice(f32[4103,512]{1,0:T(8,128)} %subtract_add_fusion.5), slice={[2:4103:2], [0:512:1]} | slice | bytes 8400896 | tf_op jit(solution)/shard_map/jvp()/slice | solution.py:58
  491.2 24.3 %fusion.28 = f32[2051,512]{1,0:T(8,128)S(1)} fusion(f32[2051,512]{1,0:T(8,128)} %slice.456, f32[2051,512]{1,0:T(8,128)} %slice.455, f32[2051,512]{1,0:T(8,128)} %slice.454, f32[8192,512]{1,0:T(8,128)} %subtract_add_fusion.4), kind=kOutput, calls=%fused_computation.59 | convolution fusion | flops 19361964032 | bytes 19978240 | tf_op jit(solution)/shard_map/jvp(bmk,bkn->bmn)/dot_general | solution.py:42
  540.8 11.6 slice.459
  552.4 11.4 slice.460
  563.8 13.5 fusion.64
  604.3 19.5 slice.466
  623.8 19.9 slice.467
  767.6 22.5 %subtract_add_fusion = f32[3,768,3072]{2,1,0:T(8,128)} fusion(bf16[3,768,3072]{2,1,0:T(8,128)(2,1)} %all-gather.23.cloned.1.call-done), kind=kLoop, calls=%fused_computation.2 | loop fusion | flops 28311552 | bytes 42467328 | tf_op jit(solution)/shard_map/add | solution.py:34
  824.4 11.8 fusion.25
  837.0 22.6 %subtract_add_fusion.1 = f32[3,768,3072]{2,1,0:T(8,128)} fusion(bf16[3,768,3072]{2,1,0:T(8,128)(2,1)} %all-gather.19.cloned.1.call-done), kind=kLoop, calls=%fused_computation.3 | loop fusion | flops 28311552 | bytes 42467328 | tf_op jit(solution)/shard_map/jvp()/add | solution.py:34
  890.9 12.8 fusion.32
  962.8 21.4 %pad_add_fusion = f32[3,768,3072]{2,1,0:T(8,128)} fusion(f32[1,768,3072]{2,1,0:T(8,128)} %pad_bitcast_fusion, f32[1,768,3072]{2,1,0:T(8,128)} %pad_bitcast_fusion.1, f32[1,768,3072]{2,1,0:T(8,128)} %convolution_bitcast_fusion.1, f32[1,768,3072]{2,1,0:T(8,128)S(1)} %convolution_bitcast_fusion.2), kind=kLoop, calls=%fused_computation.4 | loop fusion | flops 21233664 | bytes 66060288 | tf_op jit(solution)/shard_map/transpose(jvp())/add_any | solution.py:122
  984.2 19.8 slice_bitcast_fusion.2
  1052.0 11.1 copy.275
  1096.8 22.2 %pad.260 = f32[512,512]{0,1:T(8,128)} pad(f32[256,512]{0,1:T(8,128)} %get-tuple-element.231, f32[]{:T(128)} %constant.65.clone.1), padding=1_0_1x0_0_0 | pad | bytes 1572868 | tf_op jit(solution)/shard_map/transpose(jvp())/pad | solution.py:58
  1118.9 20.0 pad.261
  1190.4 16.7 pad.267
  1216.0 16.9 pad.269
  1242.8 14.2 fusion.103
  1266.9 32.8 %pad.271 = f32[4103,512]{1,0:T(8,128)} pad(f32[2051,512]{1,0:T(8,128)} %get-tuple-element.204, f32[]{:T(128)} %constant.65.clone.1), padding=2_0_1x0_0_0 | pad | bytes 12603396 | tf_op jit(solution)/shard_map/transpose(jvp())/pad | solution.py:58
  1299.7 32.6 %pad.272 = f32[4103,512]{1,0:T(8,128)} pad(f32[2051,512]{1,0:T(8,128)} %get-tuple-element.202, f32[]{:T(128)} %constant.65.clone.1), padding=1_1_1x0_0_0 | pad | bytes 12603396 | tf_op jit(solution)/shard_map/transpose(jvp())/pad | solution.py:58
  1332.2 32.5 %pad.273 = f32[4103,512]{1,0:T(8,128)} pad(f32[2051,512]{1,0:T(8,128)} %get-tuple-element.203, f32[]{:T(128)} %constant.65.clone.1), padding=0_2_1x0_0_0 | pad | bytes 12603396 | tf_op jit(solution)/shard_map/transpose(jvp())/pad | solution.py:58
  1364.7 136.0 %reduce-scatter.15.cloned.1.call-done = f32[96,3072]{1,0:T(8,128)} async-done(((f32[768,3072]{1,0:T(8,128)}), f32[96,3072]{1,0:T(8,128)}) %reduce-scatter.15.cloned.1.call-update) | async-done | bytes 1179664 | tf_op jit(solution)/shard_map/reduce_scatter | solution.py:323
  1504.9 19.7 fusion.88
  1540.2 16.8 fusion.90
  1557.1 26.4 %fusion.91 = f32[1536,512]{1,0:T(8,128)} fusion(f32[4103,512]{1,0:T(8,128)} %slice.452, f32[4103,512]{1,0:T(8,128)S(1)} %bitcast.1364, f32[4103,512]{1,0:T(8,128)S(1)} %bitcast.1362, bf16[1,4103,512]{2,1,0:T(8,128)(2,1)S(1)} %bitcast.1373), kind=kOutput, calls=%fused_computation.150 | convolution fusion | flops 38733369344 | bytes 32556032 | tf_op jit(solution)/shard_map/transpose(jvp(bmk,bkn->bmn))/dot_general | solution.py:42
  1583.4 10.6 pad_add_fusion.1
  1600.5 25.8 %fusion.85 = f32[4103,1536]{1,0:T(8,128)} fusion(bf16[1,4103,512]{2,1,0:T(8,128)(2,1)} %fusion.88, f32[8192,512]{1,0:T(8,128)} %subtract_add_fusion.4), kind=kOutput, calls=%fused_computation.141 | convolution fusion | flops 38720765952 | bytes 32557056 | tf_op jit(solution)/shard_map/transpose(jvp(bmk,bkn->bmn))/dot_general | solution.py:42
  1626.3 18.2 fusion.480
  1644.5 64.9 %pad.277 = f32[8207,512]{1,0:T(8,128)} pad(f32[4103,512]{1,0:T(8,128)} %get-tuple-element.201, f32[]{:T(128)} %constant.65.clone.1), padding=2_0_1x0_0_0 | pad | bytes 25210884 | tf_op jit(solution)/shard_map/transpose(jvp())/pad | solution.py:58
  1709.4 64.4 %pad.278 = f32[8207,512]{1,0:T(8,128)} pad(f32[4103,512]{1,0:T(8,128)} %get-tuple-element.199, f32[]{:T(128)} %constant.65.clone.1), padding=1_1_1x0_0_0 | pad | bytes 25210884 | tf_op jit(solution)/shard_map/transpose(jvp())/pad | solution.py:58
  1773.8 64.4 %pad.279 = f32[8207,512]{1,0:T(8,128)} pad(f32[4103,512]{1,0:T(8,128)} %get-tuple-element.200, f32[]{:T(128)} %constant.65.clone.1), padding=0_2_1x0_0_0 | pad | bytes 25210884 | tf_op jit(solution)/shard_map/transpose(jvp())/pad | solution.py:58
  1838.2 34.3 %fusion.55 = bf16[1,8207,512]{2,1,0:T(8,128)(2,1)} fusion(f32[8207,512]{1,0:T(8,128)} %get-tuple-element.195, f32[8207,512]{1,0:T(8,128)} %pad.279, f32[8207,512]{1,0:T(8,128)} %pad.277, f32[8207,512]{1,0:T(8,128)} %pad.278, f32[8207,512]{1,0:T(8,128)} %copy-done, bf16[1,8207,512]{2,1,0:T(8,128)(2,1)} %copy-done.2), kind=kLoop, calls=%fused_computation.94 | loop fusion | flops 79837696 | bytes 100847616 | tf_op jit(solution)/shard_map/transpose(jvp())/convert_element_type | solution.py:30
  1880.1 15.4 fusion
  1904.8 44.1 %all-reduce.72 = (f32[]{:T(128)}, f32[]{:T(128)}, f32[12,512]{1,0:T(8,128)S(1)}, f32[10,768]{1,0:T(8,128)S(1)}) all-reduce(f32[]{:T(128)S(6)} %div.229, f32[]{:T(128)S(6)} %add.751, f32[12,512]{1,0:T(8,128)S(1)} %pad_add_fusion.9, f32[10,768]{1,0:T(8,128)S(1)} %add_add_fusion.5), channel_id=1, replica_groups=mesh['dp'=8,'narrow'=4] {'dp','narrow'}, use_global_device_ids=true, to_apply=%region_22.23 | all-reduce | flops 13826 | bytes 110608 | tf_op jit(solution)/shard_map/psum | solution.py:334
  (924 shorter events, 656.8 us)
Async XLA Ops:
  7.2 26.5 %all-gather.21.cloned.1.call-start = ((), (), s32[]{:S(2)}) async-start(), calls=%async_computation.10 | async-start | bytes 2211840 | tf_op jit(solution)/shard_map/all_gather | solution.py:293
  9.3 24.5 %copy-start.235 = (s32[128]{0:T(128)S(1)}, s32[128]{0:T(128)}, u32[]{:S(2)}) copy-start(s32[128]{0:T(128)} %param.22) | copy-start | bytes 1540
  9.3 65.5 %copy-start.135 = (f32[41040]{0:T(1024)S(1)}, f32[41040]{0:T(1024)}, u32[]{:S(2)}) copy-start(f32[41040]{0:T(1024)} %param.20) | copy-start | bytes 492484
  9.3 292.2 %all-gather.17.cloned.1.call-start = ((), (), s32[]{:S(2)}) async-start(), calls=%async_computation.8 | async-start | bytes 2211840 | tf_op jit(solution)/shard_map/all_gather | solution.py:292
  11.4 86.9 %copy-start.142 = (f32[12,512]{1,0:T(8,128)S(1)}, f32[12,512]{1,0:T(8,128)}, u32[]{:S(2)}) copy-start(f32[12,512]{1,0:T(8,128)} %param.24) | copy-start | bytes 73732
  11.4 290.2 %all-gather.15.cloned.1.call-start = ((), (), s32[]{:S(2)}) async-start(), calls=%async_computation.7 | async-start | bytes 3981312 | tf_op jit(solution)/shard_map/all_gather | solution.py:299
  22.3 315.0 %all-gather.13.cloned.1.call-start = ((), (), s32[]{:S(2)}) async-start(), calls=%async_computation.6 | async-start | bytes 8650752 | tf_op jit(solution)/shard_map/all_gather | solution.py:304
  23.1 744.5 %all-gather.23.cloned.1.call-start = ((), (), s32[]{:S(2)}) async-start(), calls=%async_computation.11 | async-start | bytes 15925248 | tf_op jit(solution)/shard_map/all_gather | solution.py:298
  33.7 803.3 %all-gather.19.cloned.1.call-start = ((), (), s32[]{:S(2)}) async-start(), calls=%async_computation.9 | async-start | bytes 15925248 | tf_op jit(solution)/shard_map/all_gather | solution.py:297
  114.5 40.5 %copy-start = (f32[8207,512]{1,0:T(8,128)}, f32[8207,512]{1,0:T(8,128)S(1)}, u32[]{:S(2)}) copy-start(f32[8207,512]{1,0:T(8,128)S(1)} %fusion.404) | copy-start | bytes 50423812
  115.7 39.3 %copy-start.2 = (bf16[1,8207,512]{2,1,0:T(8,128)(2,1)}, bf16[1,8207,512]{2,1,0:T(8,128)(2,1)S(1)}, u32[]{:S(2)}) copy-start(bf16[1,8207,512]{2,1,0:T(8,128)(2,1)S(1)} %convert_bitcast_fusion) | copy-start | bytes 25211908
  254.9 41.8 %copy-start.138 = (f32[10,768]{1,0:T(8,128)S(1)}, f32[10,768]{1,0:T(8,128)}, u32[]{:S(2)}) copy-start(f32[10,768]{1,0:T(8,128)} %param.27) | copy-start | bytes 92164
  254.9 41.8 %copy-start.220 = (s32[128]{0:T(128)S(1)}, s32[128]{0:T(128)}, u32[]{:S(2)}) copy-start(s32[128]{0:T(128)} %param.21) | copy-start | bytes 1540
  254.9 42.6 %copy-start.139 = (f32[10,768]{1,0:T(8,128)S(1)}, f32[10,768]{1,0:T(8,128)}, u32[]{:S(2)}) copy-start(f32[10,768]{1,0:T(8,128)} %param.30) | copy-start | bytes 92164
  301.6 1063.1 %reduce-scatter.11.cloned.1.call-start = ((), (), s32[]{:S(2)}) async-start(), calls=%async_computation.12 | async-start | bytes 10616832 | tf_op jit(solution)/shard_map/reduce_scatter | solution.py:323
  623.8 25.9 %copy-start.54 = (f32[256,512]{0,1:T(8,128)}, f32[256,512]{0,1:T(8,128)S(1)}, u32[]{:S(2)}) copy-start(f32[256,512]{0,1:T(8,128)S(1)} %slice.466) | copy-start | bytes 1572868
  659.2 42.9 %copy-start.32 = (f32[128,768]{1,0:T(8,128)}, f32[128,768]{1,0:T(8,128)S(1)}, u32[]{:S(2)}) copy-start(f32[128,768]{1,0:T(8,128)S(1)} %get-tuple-element.175) | copy-start | bytes 1179652
  767.2 96.9 %copy-start.183 = (f32[128]{0:T(128)}, f32[128]{0:T(128)S(1)}, u32[]{:S(2)}) copy-start(f32[128]{0:T(128)S(1)} %broadcast_multiply_fusion.6) | copy-start | bytes 1540
  767.4 96.7 %copy-start.194 = (f32[128]{0:T(128)}, f32[128]{0:T(128)S(1)}, u32[]{:S(2)}) copy-start(f32[128]{0:T(128)S(1)} %fusion.431) | copy-start | bytes 1540
  767.6 96.5 %copy-start.92 = (bf16[128,768]{1,0:T(8,128)(2,1)}, bf16[128,768]{1,0:T(8,128)(2,1)S(1)}, u32[]{:S(2)}) copy-start(bf16[128,768]{1,0:T(8,128)(2,1)S(1)} %fusion.441) | copy-start | bytes 589828
  877.6 38.1 %slice-start = ((s8[28311552]{0:T(1024)(128)(4,1)}), s8[4194304]{0:T(1024)(128)(4,1)S(1)}, s32[]{:S(2)}) async-start(s8[28311552]{0:T(1024)(128)(4,1)} %bitcast.1349), calls=%async_computation.18 | async-start | bytes 8388608
  877.8 26.0 %copy-start.186 = (f32[128]{0:T(128)}, f32[128]{0:T(128)S(1)}, u32[]{:S(2)}) copy-start(f32[128]{0:T(128)S(1)} %broadcast_multiply_fusion.5) | copy-start | bytes 1540
  878.1 25.8 %copy-start.197 = (f32[128]{0:T(128)}, f32[128]{0:T(128)S(1)}, u32[]{:S(2)}) copy-start(f32[128]{0:T(128)S(1)} %fusion.432) | copy-start | bytes 1540
  878.2 37.4 %slice-start.1 = ((s8[28311552]{0:T(1024)(128)(4,1)}), s8[4194304]{0:T(1024)(128)(4,1)S(1)}, s32[]{:S(2)}) async-start(s8[28311552]{0:T(1024)(128)(4,1)} %bitcast.1349), calls=%async_computation.19 | async-start | bytes 8388608
  887.1 28.5 %slice-start.2 = ((s8[28311552]{0:T(1024)(128)(4,1)}), s8[4194304]{0:T(1024)(128)(4,1)S(1)}, s32[]{:S(2)}) async-start(s8[28311552]{0:T(1024)(128)(4,1)} %bitcast.1349), calls=%async_computation.20 | async-start | bytes 8388608
  890.9 24.7 %slice-start.3 = ((s8[28311552]{0:T(1024)(128)(4,1)}), s8[4194304]{0:T(1024)(128)(4,1)S(1)}, s32[]{:S(2)}) async-start(s8[28311552]{0:T(1024)(128)(4,1)} %bitcast.1349), calls=%async_computation.21 | async-start | bytes 8388608
  890.9 24.7 %slice-start.4 = ((s8[28311552]{0:T(1024)(128)(4,1)}), s8[4194304]{0:T(1024)(128)(4,1)S(1)}, s32[]{:S(2)}) async-start(s8[28311552]{0:T(1024)(128)(4,1)} %bitcast.1349), calls=%async_computation.22 | async-start | bytes 8388608
  1004.0 360.7 %reduce-scatter.13.cloned.1.call-start = ((), (), s32[]{:S(2)}) async-start(), calls=%async_computation.13 | async-start | bytes 10616832 | tf_op jit(solution)/shard_map/reduce_scatter | solution.py:323
  1004.8 495.9 %reduce-scatter.15.cloned.1.call-start = ((), (), s32[]{:S(2)}) async-start(), calls=%async_computation.14 | async-start | bytes 10616832 | tf_op jit(solution)/shard_map/reduce_scatter | solution.py:323
  1005.5 872.9 %reduce-scatter.21.cloned.1.call-start = ((), (), s32[]{:S(2)}) async-start(), calls=%async_computation.17 | async-start | bytes 7962624
  1084.8 814.3 %reduce-scatter.17.cloned.1.call-start = ((), (), s32[]{:S(2)}) async-start(), calls=%async_computation.15 | async-start | bytes 4423680 | tf_op jit(solution)/shard_map/reduce_scatter | solution.py:328
  1093.0 46.0 %copy-start.19 = (f32[512,512]{0,1:T(8,128)S(1)}, f32[512,512]{0,1:T(8,128)}, u32[]{:S(2)}) copy-start(f32[512,512]{0,1:T(8,128)} %copy-done.18) | copy-start | bytes 3145732
  1093.0 46.0 %copy-start.36 = (f32[512,512]{0,1:T(8,128)S(1)}, f32[512,512]{0,1:T(8,128)}, u32[]{:S(2)}) copy-start(f32[512,512]{0,1:T(8,128)} %copy-done.35) | copy-start | bytes 3145732
  1093.0 45.9 %copy-start.44 = (bf16[1,512,512]{1,2,0:T(8,128)(2,1)S(1)}, bf16[1,512,512]{1,2,0:T(8,128)(2,1)}, u32[]{:S(2)}) copy-start(bf16[1,512,512]{1,2,0:T(8,128)(2,1)} %copy-done.43) | copy-start | bytes 1572868
  1148.5 26.4 %copy-start.15 = (f32[1025,512]{1,0:T(8,128)S(1)}, f32[1025,512]{1,0:T(8,128)}, u32[]{:S(2)}) copy-start(f32[1025,512]{1,0:T(8,128)} %copy-done.14) | copy-start | bytes 6297604
  1148.5 26.4 %copy-start.24 = (bf16[1,1025,512]{2,1,0:T(8,128)(2,1)S(1)}, bf16[1,1025,512]{2,1,0:T(8,128)(2,1)}, u32[]{:S(2)}) copy-start(bf16[1,1025,512]{2,1,0:T(8,128)(2,1)} %copy-done.23) | copy-start | bytes 3148804
  1504.9 397.5 %reduce-scatter.19.cloned.1.call-start = ((), (), s32[]{:S(2)}) async-start(), calls=%async_computation.16 | async-start | bytes 17301504 | tf_op jit(solution)/shard_map/reduce_scatter | solution.py:333
  1530.7 26.2 %slice-start.10 = ((s8[8404992]{0:T(1024)(128)(4,1)}), s8[4194304]{0:T(1024)(128)(4,1)S(1)}, s32[]{:S(2)}) async-start(s8[8404992]{0:T(1024)(128)(4,1)} %bitcast.1361), calls=%async_computation.28 | async-start | bytes 8388608
  1530.8 26.2 %slice-start.11 = ((s8[8404992]{0:T(1024)(128)(4,1)}), s8[4194304]{0:T(1024)(128)(4,1)S(1)}, s32[]{:S(2)}) async-start(s8[8404992]{0:T(1024)(128)(4,1)} %bitcast.1361), calls=%async_computation.29 | async-start | bytes 8388608
  1530.8 26.2 %slice-start.13 = ((s8[8404992]{0:T(1024)(128)(4,1)}), s8[4194304]{0:T(1024)(128)(4,1)S(1)}, s32[]{:S(2)}) async-start(s8[8404992]{0:T(1024)(128)(4,1)} %bitcast.1363), calls=%async_computation.31 | async-start | bytes 8388608
  1530.8 26.2 %slice-start.14 = ((s8[8404992]{0:T(1024)(128)(4,1)}), s8[4194304]{0:T(1024)(128)(4,1)S(1)}, s32[]{:S(2)}) async-start(s8[8404992]{0:T(1024)(128)(4,1)} %bitcast.1363), calls=%async_computation.32 | async-start | bytes 8388608
  1530.8 26.2 %slice-start.16 = ((s8[4202496]{0:T(1024)(128)(4,1)}), s8[4194304]{0:T(1024)(128)(4,1)S(1)}, s32[]{:S(2)}) async-start(s8[4202496]{0:T(1024)(128)(4,1)} %bitcast.1372), calls=%async_computation.34 | async-start | bytes 8388608
  1838.2 34.3 %copy-start.49 = (f32[8207,10]{0,1:T(8,128)S(1)}, f32[8207,10]{0,1:T(8,128)}, u32[]{:S(2)}) copy-start(f32[8207,10]{0,1:T(8,128)} %copy-done.48) | copy-start | bytes 984844
  1872.6 24.3 %copy-start.214 = (f32[512]{0:T(512)S(1)}, f32[512]{0:T(512)}, u32[]{:S(2)}) copy-start(f32[512]{0:T(512)} %get-tuple-element.101) | copy-start | bytes 6148
  1872.6 24.3 %copy-start.215 = (f32[512]{0:T(512)S(1)}, f32[512]{0:T(512)}, u32[]{:S(2)}) copy-start(f32[512]{0:T(512)} %get-tuple-element.110) | copy-start | bytes 6148
  1878.4 73.8 %copy-start.130 = (f32[3,96,768]{2,1,0:T(8,128)S(1)}, f32[3,96,768]{2,1,0:T(8,128)}, u32[]{:S(2)}) copy-start(f32[3,96,768]{2,1,0:T(8,128)} %param.39) | copy-start | bytes 2654212
  1895.5 2.1 collective-permute-start
  1898.4 53.8 %copy-start.77 = (f32[96,596]{0,1:T(8,128)}, f32[96,596]{0,1:T(8,128)S(1)}, u32[]{:S(2)}) copy-start(f32[96,596]{0,1:T(8,128)S(1)} %concatenate.34) | copy-start | bytes 686596
  (220 other events, 1464.2 us)
Sparse Core Ops, SparseCore 0:
  10.2 23.4 all-gather.20
  35.8 20.9 all-gather.16
  59.5 65.1 all-gather.14
  128.0 76.0 all-gather.12
  206.2 194.1 all-gather.22
  402.5 193.7 all-gather.18
  1004.1 164.3 reduce-scatter.10
  1172.1 162.5 reduce-scatter.12
  1338.3 162.3 reduce-scatter.14
  1504.2 128.0 reduce-scatter.20
  1635.1 39.4 reduce-scatter.16
  1676.8 182.9 reduce-scatter.18
